TPU v7x, 256 devices: a whole 4x4x8 slice. The times are simulated.
256 devices in a mesh: seq: 64 (over y, z, core), grp: 4 (over x).
Axes of the slice: x: 4, y: 4, z: 8, core: 2. Of those that a mesh axis runs over, the one named last changes fastest.
Arguments:
- doc_lengths: int32 [4, 16], P('grp'), may hold values from 1 to 1024, 8192 in all within a row
- hidden: bfloat16 [4, 8192, 7168], P('grp', 'seq'), may hold values from -16 to 16
- gate_weight: bfloat16 [7168, 64], P(('seq', 'grp')), may hold values from -0.0625 to 0.0625
- target_query: bfloat16 [4, 8192, 36864], P('grp', 'seq'), may hold values from -30 to 30
- latent_keys: bfloat16 [4, 8192, 576], P('grp', 'seq'), may hold values from -6 to 6
- index_query: bfloat16 [4, 8192, 8192], P('grp', 'seq'), may hold values from -15 to 15
- index_keys: bfloat16 [4, 8192, 128], P('grp', 'seq'), may hold values from -6 to 6
Outputs:
- divergence: float32 [4, 8192], P('grp', 'seq')
- grad_gate: float32 [7168, 64], P(('seq', 'grp'))
All inputs are finite; a program needn't handle non-finite values.
Results may differ from a plain program's by a relative error of at most 0.0022.
Values may be sent and summed in bfloat16 or wider, within the bound.
A program may use at most 128 MiB of HBM per device.

v0:
```python
import jax
import jax.numpy as jnp
from jax import lax
from jax.sharding import Mesh
from jax.sharding import PartitionSpec as P

LOOK = 8
SEQ = ("seq_0", "seq_1", "seq_2")
SEQ_GRP = ("seq_0", "seq_1", "seq_2", "grp")
target_scale = 0.07216878364870322
highest = lax.Precision.HIGHEST
floor_value = -1e30


def shifted(block, axis, distance):
    devices = range(lax.axis_size(axis))
    route = [(i - distance, i) for i in devices if i - distance in devices]
    return lax.ppermute(block, axis, route)


def reduced_to_own(blocks, axes, sequence):
    inside = blocks.shape[1:]
    blocks = blocks.reshape(*(lax.axis_size(a) for a in axes), *inside)
    blocks = jnp.moveaxis(blocks, sequence, range(len(axes))).reshape(-1, *inside)
    for k in sequence:
        blocks = lax.psum_scatter(blocks, axes[k], scatter_dimension=0, tiled=True)
    return blocks[0]


def split_up(value, dim, peers):
    lengths = value.shape
    blocks = value.reshape(*lengths[:dim], peers, lengths[dim] // peers, *lengths[dim + 1 :])
    return jnp.moveaxis(blocks, dim, 0)


def scatter_axes(value, axes, sequence, dim):
    peers = lax.axis_size(axes)
    return reduced_to_own(split_up(value, dim, peers), axes, sequence)


def piece_terms(
    target_rows,
    index_rows,
    gate_rows,
    latent_panel,
    index_panel,
    panel_start_offset,
    positions,
    lengths,
    doc_most,
):
    piece_count, piece_rows = positions.shape
    latent_width = latent_panel.shape[1]
    index_width = index_panel.shape[1]
    key_tile = 128
    span_keys = (doc_most + piece_rows - 1 + key_tile - 1) // key_tile * key_tile
    doc_ends = jnp.cumsum(lengths)
    starts = jnp.sum(lengths * (doc_ends <= positions[..., None]).astype(jnp.int32), -1)
    tile_counts = (positions[:, -1] + 1 - starts[:, 0] + key_tile - 1) // key_tile
    ranking = jnp.argsort(tile_counts, stable=True)
    batch_pieces = max(1, 16 // piece_rows)
    batch_count = piece_count // batch_pieces
    factor = index_width ** (-0.5)
    latent_padded = jnp.concatenate(
        [latent_panel, jnp.zeros((key_tile, latent_width), latent_panel.dtype)], 0
    )
    index_padded = jnp.concatenate(
        [index_panel, jnp.zeros((key_tile, index_width), index_panel.dtype)], 0
    )
    offsets = jnp.arange(key_tile, dtype=jnp.int32)

    def one_batch(batch_index):
        chosen = lax.dynamic_slice_in_dim(ranking, batch_index * batch_pieces, batch_pieces, 0)
        queries = jnp.take(target_rows, chosen, axis=0).reshape(
            batch_pieces, piece_rows, -1, latent_width
        )
        indexer_query_rows = jnp.take(index_rows, chosen, axis=0).reshape(
            batch_pieces, piece_rows, -1, index_width
        )
        gate_values = jnp.take(gate_rows, chosen, axis=0)
        row_pos = jnp.take(positions, chosen, axis=0)
        row_start = jnp.take(starts, chosen, axis=0)
        anchor = row_start[:, 0]
        turn_count = jnp.max(jnp.take(tile_counts, chosen, axis=0))
        head_count = queries.shape[2]
        gate_heads = gate_values.shape[2]

        def allowed_of(turn_index):
            key_pos = anchor[:, None] + turn_index * key_tile + offsets[None, :]
            return (key_pos[:, None, :] >= row_start[:, :, None]) & (
                key_pos[:, None, :] <= row_pos[:, :, None]
            )

        def cut_panel(first_key):
            return (
                lax.dynamic_slice_in_dim(
                    latent_padded, first_key - panel_start_offset, key_tile, 0
                ),
                lax.dynamic_slice_in_dim(index_padded, first_key - panel_start_offset, key_tile, 0),
            )

        def first_pass(turn_index, carry):
            logit_store, relu_store, head_peak, head_total, score_peak, score_total = carry
            latent_tile, indexer_key_block = jax.vmap(cut_panel)(anchor + turn_index * key_tile)
            allowed = allowed_of(turn_index)
            logits = (
                jnp.einsum(
                    "brhc,bkc->brhk", queries, latent_tile, preferred_element_type=jnp.float32
                )
                * target_scale
            )
            relu_score = jnp.maximum(
                jnp.einsum(
                    "fjme,fve->fjmv",
                    indexer_query_rows,
                    indexer_key_block,
                    preferred_element_type=jnp.float32,
                ),
                0.0,
            )
            score = factor * jnp.einsum("brh,brhk->brk", gate_values, relu_score, precision=highest)
            masked = jnp.where(allowed[:, :, None, :], logits, floor_value)
            new_peak = jnp.maximum(head_peak, jnp.max(masked, -1))
            head_total = head_total * jnp.exp(head_peak - new_peak) + jnp.sum(
                jnp.where(allowed[:, :, None, :], jnp.exp(masked - new_peak[..., None]), 0.0), -1
            )
            masked_score = jnp.where(allowed, score, floor_value)
            new_score_peak = jnp.maximum(score_peak, jnp.max(masked_score, -1))
            score_total = score_total * jnp.exp(score_peak - new_score_peak) + jnp.sum(
                jnp.where(allowed, jnp.exp(masked_score - new_score_peak[..., None]), 0.0), -1
            )
            logit_store = lax.dynamic_update_slice_in_dim(
                logit_store, logits, turn_index * key_tile, 3
            )
            relu_store = lax.dynamic_update_slice_in_dim(
                relu_store, relu_score, turn_index * key_tile, 3
            )
            return (logit_store, relu_store, new_peak, head_total, new_score_peak, score_total)

        start_carry = (
            jnp.zeros((batch_pieces, piece_rows, head_count, span_keys), jnp.float32),
            jnp.zeros((batch_pieces, piece_rows, gate_heads, span_keys), jnp.float32),
            jnp.full((batch_pieces, piece_rows, head_count), floor_value, jnp.float32),
            jnp.zeros((batch_pieces, piece_rows, head_count), jnp.float32),
            jnp.full((batch_pieces, piece_rows), floor_value, jnp.float32),
            jnp.zeros((batch_pieces, piece_rows), jnp.float32),
        )
        logit_store, relu_store, head_peak, head_total, score_peak, score_total = lax.fori_loop(
            0, turn_count, first_pass, start_carry
        )
        head_log = head_peak + jnp.log(head_total)
        score_log = score_peak + jnp.log(score_total)

        def second_pass(turn_index, carry):
            row_div, delta_terms = carry
            allowed = allowed_of(turn_index)
            logits = lax.dynamic_slice_in_dim(logit_store, turn_index * key_tile, key_tile, 3)
            relu_score = lax.dynamic_slice_in_dim(relu_store, turn_index * key_tile, key_tile, 3)
            probabilities = jnp.where(
                allowed[:, :, None, :], jnp.exp(logits - head_log[..., None]), 0.0
            )
            target = jnp.mean(probabilities, axis=2)
            score = factor * jnp.einsum("brh,brhk->brk", gate_values, relu_score, precision=highest)
            log_model = jnp.where(allowed, score - score_log[..., None], 0.0)
            model_prob = jnp.where(allowed, jnp.exp(log_model), 0.0)
            positive = target > 0
            target_log_probabilities = jnp.where(
                positive, target * jnp.log(jnp.where(positive, target, 1.0)), 0.0
            )
            row_div = row_div + jnp.sum(
                jnp.where(allowed, target_log_probabilities - target * log_model, 0.0), -1
            )
            delta_terms = delta_terms + factor * jnp.einsum(
                "brk,brhk->brh", model_prob - target, relu_score, precision=highest
            )
            return (row_div, delta_terms)

        return lax.fori_loop(
            0,
            turn_count,
            second_pass,
            (
                jnp.zeros((batch_pieces, piece_rows), jnp.float32),
                jnp.zeros((batch_pieces, piece_rows, gate_heads), jnp.float32),
            ),
        )

    sorted_div, sorted_delta = lax.map(one_batch, jnp.arange(batch_count, dtype=jnp.int32))
    sorted_div = sorted_div.reshape(piece_count, piece_rows)
    sorted_delta = sorted_delta.reshape(piece_count, piece_rows, -1)
    row_div = jnp.zeros_like(sorted_div).at[ranking].set(sorted_div)
    delta_terms = jnp.zeros_like(sorted_delta).at[ranking].set(sorted_delta)
    return (row_div, delta_terms)


def body(doc_lengths, hidden, gate_weight, target_query, latent_keys, index_query, index_keys):
    seq_count = lax.axis_size(SEQ)
    my_index = lax.axis_index(SEQ)
    row_count = hidden.shape[1]
    reach_devices = min(LOOK, seq_count // 2)
    doc_most = reach_devices * row_count
    lengths = doc_lengths[0]
    full_gate = lax.all_gather(gate_weight, SEQ_GRP, axis=0, tiled=True)
    block_rows = 16
    block_count = row_count // block_rows
    latent_parts = []
    index_parts = []
    for offset in range(reach_devices, 0, -1):
        latent_prev, index_prev = shifted((latent_keys[0], index_keys[0]), SEQ, offset)
        latent_parts.append(latent_prev)
        index_parts.append(index_prev)
    latent_win = jnp.concatenate(latent_parts + [latent_keys[0]], 0)
    index_win = jnp.concatenate(index_parts + [index_keys[0]], 0)
    panel_start_offset = my_index * row_count - doc_most
    positions = (my_index * row_count + jnp.arange(row_count, dtype=jnp.int32)).reshape(
        block_count, block_rows
    )
    gates_home = jnp.dot(hidden[0], full_gate, preferred_element_type=jnp.float32).reshape(
        block_count, block_rows, -1
    )
    row_div, delta_terms = piece_terms(
        target_query[0].reshape(block_count, block_rows, -1),
        index_query[0].reshape(block_count, block_rows, -1),
        gates_home,
        latent_win,
        index_win,
        panel_start_offset,
        positions,
        lengths,
        doc_most,
    )
    gate_delta = (delta_terms.reshape(row_count, -1) / row_count).astype(jnp.bfloat16)
    partial_value = jnp.dot(hidden[0].T, gate_delta, preferred_element_type=jnp.float32)
    divergence = row_div.reshape(1, row_count)
    grad_gate = scatter_axes(partial_value, SEQ_GRP, (2, 0, 1, 3), 0)
    return (divergence, grad_gate)


def solution(mesh):
    split = Mesh(
        mesh.devices.reshape(4, 8, 2, mesh.shape["grp"]), ("seq_0", "seq_1", "seq_2", "grp")
    )
    in_specs = (
        P("grp", None),
        P("grp", SEQ, None),
        P(SEQ_GRP, None),
        P("grp", SEQ, None),
        P("grp", SEQ, None),
        P("grp", SEQ, None),
        P("grp", SEQ, None),
    )
    out_specs = (P("grp", SEQ), P(SEQ_GRP, None))
    return jax.shard_map(body, mesh=split, in_specs=in_specs, out_specs=out_specs, check_vma=False)
```

profile of v0, /device:TPU:8, one launch (start us, length us, event | category | flops | bytes accessed | tf_op | source)
XLA Modules:
  0.0 1303.6 jit_solution(13120426017892355332)
XLA Ops:
  7.2 9.2 collective-permute-start
  16.5 3.0 collective-permute-start.1
  19.5 3.0 collective-permute-start.2
  22.5 7.1 collective-permute-start.3
  29.6 2.7 collective-permute-start.8
  34.3 134.9 %all-gather = bf16[256,28,64]{2,1,0:T(8,128)(2,1)} all-gather(bf16[1,28,64]{2,1,0:T(8,128)(2,1)} %bitcast.295), channel_id=1, replica_groups=mesh['seq_0'=4,'seq_1'=8,'seq_2'=2,'grp'=4] {'seq_0','seq_1','seq_2','grp'}, dimensions={0}, use_global_device_ids=true | all-gather | bytes 921088 | tf_op jit(solution)/shard_map/all_gather | solution.py:203
  169.3 4.0 reshape.564
  176.4 3.7 collective-permute-start.9
  180.1 6.6 collective-permute-done.9
  188.7 7.8 collective-permute-done.10
  198.4 7.2 collective-permute-done.11
  207.5 6.9 collective-permute-done.12
  216.3 6.3 collective-permute-done.13
  224.6 6.0 collective-permute-done.14
  232.5 5.4 collective-permute-done.15
  246.7 3.8 collective-permute-done.4
  257.5 263.1 %while.59 = (s32[]{:T(128)}, f32[8,1,16]{2,1,0:T(1,128)S(1)}, f32[8,1,16,64]{3,2,1,0:T(8,128)}, s32[8]{0:T(128)S(1)}, s32[8]{0:T(128)S(1)}, /*index=5*/s32[8]{0:...) while((s32[]{:T(128)}, f32[8,1,16]{2,1,0:T(1,128)S(1)}, ...), condition=%wide.region_14.16_spmd.clone.clone, body=%wide.region_3.15_spmd.clone.clone.sunk | while | flops 191511280 | bytes 22292232 | solution.py:188
  265.2 2.7 select_n.240
  270.3 2.6 broadcast.479
  272.9 2.7 broadcast.479.clone
  275.6 6.1 while.60
  281.7 5.2 while.61
  295.2 2.7 select_n.240
  300.3 2.6 broadcast.479
  303.0 2.7 broadcast.479.clone
  305.6 6.1 while.60
  311.8 5.2 while.61
  325.3 2.7 select_n.240
  330.4 2.6 broadcast.479
  333.0 2.7 broadcast.479.clone
  335.7 6.1 while.60
  341.9 5.2 while.61
  355.3 2.7 select_n.240
  360.5 2.6 broadcast.479
  363.1 2.7 broadcast.479.clone
  365.8 6.1 while.60
  371.9 5.2 while.61
  385.4 2.7 select_n.240
  390.5 2.6 broadcast.479
  393.2 2.7 broadcast.479.clone
  395.8 6.1 while.60
  402.0 5.2 while.61
  415.5 2.7 select_n.240
  420.6 2.6 broadcast.479
  423.2 2.7 broadcast.479.clone
  425.9 6.1 while.60
  432.1 5.2 while.61
  445.6 2.7 select_n.240
  450.7 2.6 broadcast.479
  453.3 2.7 broadcast.479.clone
  456.0 12.2 while.60
  468.2 10.4 while.61
  486.9 2.7 select_n.240
  492.0 2.6 broadcast.479
  494.7 2.7 broadcast.479.clone
  497.3 12.2 while.60
  509.6 10.4 while.61
  523.8 3.5 copy.25
  527.3 4.6 reshape_reshape.3
  531.9 6.4 copy.26
  538.4 629.2 %reduce-scatter.5.cloned.1.call-done = f32[128,28,64]{2,0,1:T(8,128)} async-done(((f32[256,28,64]{2,0,1:T(8,128)}), f32[128,28,64]{2,0,1:T(8,128)}) %reduce-scatter.5.cloned.1.call-update) | async-done | bytes 917520 | tf_op jit(solution)/shard_map/reduce_scatter | solution.py:26
  1167.7 32.7 %reduce-scatter.7.cloned.1.call-done = f32[32,28,64]{2,0,1:T(8,128)} async-done(((f32[128,28,64]{2,0,1:T(8,128)}), f32[32,28,64]{2,0,1:T(8,128)}) %reduce-scatter.7.cloned.1.call-update) | async-done | bytes 229392 | tf_op jit(solution)/shard_map/reduce_scatter | solution.py:26
  1203.5 73.9 %all-reduce.4.cloned.1.call-done = f32[32,28,64]{2,0,1:T(8,128)} async-done(((f32[32,28,64]{2,0,1:T(8,128)}), f32[32,28,64]{2,0,1:T(8,128)}) %all-reduce.4.cloned.1.call-update) | async-done | bytes 229392
  1278.3 17.5 %all-reduce.1 = f32[4,28,64]{2,0,1:T(4,128)S(1)} all-reduce(f32[4,28,64]{2,0,1:T(4,128)S(1)} %constant_dynamic-slice_fusion.3), channel_id=5, replica_groups=mesh['seq_0'=4,'seq_1'=8,'seq_2'=2,'grp'=4] {'grp'}, use_global_device_ids=true, to_apply=%region_20.22.clone | all-reduce | flops 7168 | bytes 57344
  (473 shorter events, 199.2 us)
Async XLA Ops:
  7.2 167.0 %copy-start = (bf16[1,128,7168]{2,1,0:T(8,128)(2,1)S(1)}, bf16[1,128,7168]{2,1,0:T(8,128)(2,1)}, u32[]{:S(2)}) copy-start(bf16[1,128,7168]{2,1,0:T(8,128)(2,1)} %param.16) | copy-start | bytes 5505028
  7.2 1160.4 %reduce-scatter.5.cloned.1.call-start = ((), (), s32[]{:S(2)}) async-start(), calls=%async_computation.2 | async-start | bytes 5505024 | tf_op jit(solution)/shard_map/reduce_scatter | solution.py:26
  7.2 232.6 %collective-permute-start = (bf16[128,576]{0,1:T(8,128)(2,1)}, bf16[128,576]{0,1:T(8,128)(2,1)S(1)}, u32[]{:S(2)}, u32[]{:S(2)}) collective-permute-start(bf16[128,576]{0,1:T(8,128)(2,1)} %bitcast.276), channel_id=1, source_target_pairs={{0,32},{4,36},{8,40},{12,44},{16,48},{20,52},{24,56},{28,60},{32,6... | collective-permute-start | bytes 442376 | tf_op jit(solution)/shard_map/ppermute | solution.py:18
  16.5 226.1 %collective-permute-start.1 = (bf16[128,576]{0,1:T(8,128)(2,1)}, bf16[128,576]{0,1:T(8,128)(2,1)S(1)}, u32[]{:S(2)}, u32[]{:S(2)}) collective-permute-start(bf16[128,576]{0,1:T(8,128)(2,1)} %bitcast.277), channel_id=1, source_target_pairs={{0,28},{4,32},{8,36},{12,40},{16,44},{20,48},{24,52},{28,56},{32,6... | collective-permute-start | bytes 442376 | tf_op jit(solution)/shard_map/ppermute | solution.py:18
  19.5 225.0 %collective-permute-start.2 = (bf16[128,576]{0,1:T(8,128)(2,1)}, bf16[128,576]{0,1:T(8,128)(2,1)S(1)}, u32[]{:S(2)}, u32[]{:S(2)}) collective-permute-start(bf16[128,576]{0,1:T(8,128)(2,1)} %bitcast.278), channel_id=1, source_target_pairs={{0,24},{4,28},{8,32},{12,36},{16,40},{20,44},{24,48},{28,52},{32,5... | collective-permute-start | bytes 442376 | tf_op jit(solution)/shard_map/ppermute | solution.py:18
  22.5 224.2 %collective-permute-start.3 = (bf16[128,576]{0,1:T(8,128)(2,1)}, bf16[128,576]{0,1:T(8,128)(2,1)S(1)}, u32[]{:S(2)}, u32[]{:S(2)}) collective-permute-start(bf16[128,576]{0,1:T(8,128)(2,1)} %bitcast.279), channel_id=1, source_target_pairs={{0,20},{4,24},{8,28},{12,32},{16,36},{20,40},{24,44},{28,48},{32,5... | collective-permute-start | bytes 442376 | tf_op jit(solution)/shard_map/ppermute | solution.py:18
  29.6 146.8 %collective-permute-start.8 = (bf16[128,128]{1,0:T(8,128)(2,1)}, bf16[128,128]{1,0:T(8,128)(2,1)S(1)}, u32[]{:S(2)}, u32[]{:S(2)}) collective-permute-start(bf16[128,128]{1,0:T(8,128)(2,1)} %bitcast.286), channel_id=1, source_target_pairs={{0,32},{4,36},{8,40},{12,44},{16,48},{20,52},{24,56},{28,60},{32,6... | collective-permute-start | bytes 98312 | tf_op jit(solution)/shard_map/ppermute | solution.py:18
  174.2 2.2 copy-start.4
  174.2 63.7 %copy-start.3 = (bf16[1,128,576]{1,2,0:T(8,128)(2,1)S(1)}, bf16[1,128,576]{1,2,0:T(8,128)(2,1)}, u32[]{:S(2)}) copy-start(bf16[1,128,576]{1,2,0:T(8,128)(2,1)} %param.19) | copy-start | bytes 442372
  176.4 10.3 collective-permute-start.9
  186.8 9.7 collective-permute-start.10
  196.5 9.1 collective-permute-start.11
  205.6 8.8 collective-permute-start.12
  214.4 8.2 collective-permute-start.13
  222.6 7.9 collective-permute-start.14
  230.5 7.3 collective-permute-start.15
  237.9 12.6 collective-permute-start.4
  239.8 0.7 copy-start.2
  240.6 12.0 collective-permute-start.5
  242.5 12.4 collective-permute-start.6
  244.5 11.7 collective-permute-start.7
  256.4 1.1 copy-start.1
  538.3 662.1 %copy-start.6 = (u32[256]{0:T(256)S(1)}, u32[256]{0:T(256)}, u32[]{:S(2)}) copy-start(u32[256]{0:T(256)} %constant.381) | copy-start | bytes 3076
  538.3 662.7 %copy-start.5 = (u32[256]{0:T(256)S(1)}, u32[256]{0:T(256)}, u32[]{:S(2)}) copy-start(u32[256]{0:T(256)} %constant.385) | copy-start | bytes 3076
  538.4 662.1 %reduce-scatter.7.cloned.1.call-start = ((), (), s32[]{:S(2)}) async-start(), calls=%async_computation.3 | async-start | bytes 2293760 | tf_op jit(solution)/shard_map/reduce_scatter | solution.py:26
  1167.6 109.7 %all-reduce.4.cloned.1.call-start = ((), (), s32[]{:S(2)}) async-start(), calls=%async_computation.4 | async-start | bytes 917504
Sparse Core Ops, SparseCore 0:
  538.5 629.1 reduce-scatter.4
  1170.2 30.1 reduce-scatter.6
  1202.7 74.5 all-reduce.3
where the time goes:
time: 1320 us; the launch traced here: 1300 us
  waiting for transfers between devices  791 us (60%)
  blocking collectives  152 us (12%)
  local copies, waits for them, and re-layouts  112 us (8%)
  matrix products  87.8 us (7%)
  other arithmetic  56.2 us (4%)
  starting transfers between devices  48.1 us (4%)
  loops' own time  40.7 us (3%)
  between operations  14.9 us (1%)
    reduce_scatter x2, waiting for transfers between devices, reduced_to_own(): blocks = lax.psum_scatter(blocks, axes[k], scatter_dimension=0, tiled=True)  662 us
    all_gather x1, blocking collectives, body(): full_gate = lax.all_gather(gate_weight, SEQ_GRP, axis=0, tiled=True)  135 us
    unnamed x4, waiting for transfers between devices  74 us
    ppermute x16, waiting for transfers between devices, shifted(): return lax.ppermute(block, axis, route)  55.6 us
    ppermute x16, starting transfers between devices, shifted(): return lax.ppermute(block, axis, route)  48 us
    another operation x65, local copies, waits for them, and re-layouts  43.1 us
    another operation x1, loops' own time, piece_terms(): lax.map(one_batch, jnp.arange(batch_count, dtype=jnp.int32))  38.1 us
  transfers between devices with their start and end apart: 19, of which 14 were waited for; matrix products, arithmetic and copies ran while one was open for 1% of the time, Pallas kernels for 0%

commit v1 on v0

--- a/solution.py
+++ b/solution.py
@@ -200,7 +200,9 @@
     reach_devices = min(LOOK, seq_count // 2)
     doc_most = reach_devices * row_count
     lengths = doc_lengths[0]
-    full_gate = lax.all_gather(gate_weight, SEQ_GRP, axis=0, tiled=True)
+    full_gate = jnp.concatenate(
+        lax.all_to_all(jnp.stack([gate_weight] * lax.axis_size(SEQ_GRP)), SEQ_GRP, 0, 0), axis=0
+    )
     block_rows = 16
     block_count = row_count // block_rows
     latent_parts = []

time: 1320 us -> 1220 us (0.924)
  blocking collectives: 152 us -> 17.5 us
  local copies, waits for them, and re-layouts: 112 us -> 126 us
  starting transfers between devices: 48.1 us -> 62.1 us
    all_gather x1 -> x0, blocking collectives: 135 us -> none  [body(): full_gate = lax.all_gather(gate_weight, SEQ_GRP, axis=0, tiled=True)]
    another operation x65 -> x66, local copies, waits for them, and re-layouts: 43.1 us -> 44.7 us
  transfers between devices with their start and end apart: 19 -> 20, of which waited for: 14 -> 14; matrix products, arithmetic and copies ran while one was open for 1% -> 2% of each run, Pallas kernels for 0% -> 0%
where the time goes in v1:
time: 1220 us; the launch traced here: 1210 us
  waiting for transfers between devices  802 us (66%)
  local copies, waits for them, and re-layouts  126 us (10%)
  matrix products  87.8 us (7%)
  starting transfers between devices  62.1 us (5%)
  other arithmetic  55.5 us (5%)
  loops' own time  40.7 us (3%)
  blocking collectives  17.5 us (1%)
  between operations  14.8 us (1%)
    reduce_scatter x2, waiting for transfers between devices, reduced_to_own(): blocks = lax.psum_scatter(blocks, axes[k], scatter_dimension=0, tiled=True)  665 us
    unnamed x4, waiting for transfers between devices  74 us
    ppermute x16, waiting for transfers between devices, shifted(): return lax.ppermute(block, axis, route)  63 us
    ppermute x16, starting transfers between devices, shifted(): return lax.ppermute(block, axis, route)  50.3 us
    another operation x65, local copies, waits for them, and re-layouts  42.4 us
    another operation x1, loops' own time, piece_terms(): lax.map(one_batch, jnp.arange(batch_count, dtype=jnp.int32))  38.1 us
  transfers between devices with their start and end apart: 20, of which 14 were waited for; matrix products, arithmetic and copies ran while one was open for 2% of the time, Pallas kernels for 0%

profile of v1, /device:TPU:8, one launch (start us, length us, event | category | flops | bytes accessed | tf_op | source)
XLA Modules:
  0.0 1206.7 jit_solution(7609965194241040869)
XLA Ops:
  7.2 9.2 collective-permute-start
  16.4 3.0 collective-permute-start.1
  19.4 3.0 collective-permute-start.2
  22.4 7.1 collective-permute-start.3
  29.6 2.7 collective-permute-start.8
  34.6 4.4 reshape.591
  39.0 11.7 all-to-all-start
  52.5 5.6 collective-permute-start.9
  58.9 18.4 %collective-permute-done.9 = bf16[128,128]{1,0:T(8,128)(2,1)S(1)} collective-permute-done((bf16[128,128]{1,0:T(8,128)(2,1)S(1)}, bf16[128,128]{1,0:T(8,128)(2,1)S(1)}, u32[]{:S(2)}, u32[]{:S(2)}) %collective-permute-start.9) | collective-permute-done | bytes 32800 | tf_op jit(solution)/shard_map/ppermute | solution.py:18
  79.2 7.8 collective-permute-done.10
  88.9 7.2 collective-permute-done.11
  98.1 6.9 collective-permute-done.12
  106.9 6.3 collective-permute-done.13
  115.5 5.6 collective-permute-done.14
  123.0 5.4 collective-permute-done.15
  151.1 4.0 reshape.364
  157.2 263.2 %while.59 = (s32[]{:T(128)}, f32[8,1,16]{2,1,0:T(1,128)S(1)}, f32[8,1,16,64]{3,2,1,0:T(8,128)}, s32[8]{0:T(128)S(1)}, s32[8]{0:T(128)S(1)}, /*index=5*/s32[8]{0:...) while((s32[]{:T(128)}, f32[8,1,16]{2,1,0:T(1,128)S(1)}, ...), condition=%wide.region_14.16_spmd.clone.clone, body=%wide.region_3.15_spmd.clone.clone.sunk | while | flops 191511280 | bytes 22292232 | solution.py:188
  164.9 2.7 select_n.240
  170.0 2.6 broadcast.481
  172.6 2.7 broadcast.481.clone
  175.3 6.1 while.60
  181.5 5.2 while.61
  195.0 2.7 select_n.240
  200.1 2.6 broadcast.481
  202.7 2.7 broadcast.481.clone
  205.4 6.1 while.60
  211.5 5.2 while.61
  225.0 2.7 select_n.240
  230.1 2.6 broadcast.481
  232.8 2.7 broadcast.481.clone
  235.4 6.1 while.60
  241.6 5.2 while.61
  255.1 2.7 select_n.240
  260.2 2.6 broadcast.481
  262.8 2.7 broadcast.481.clone
  265.5 6.1 while.60
  271.7 5.2 while.61
  285.2 2.7 select_n.240
  290.3 2.6 broadcast.481
  292.9 2.7 broadcast.481.clone
  295.6 6.1 while.60
  301.8 5.2 while.61
  315.2 2.7 select_n.240
  320.4 2.6 broadcast.481
  323.0 2.7 broadcast.481.clone
  325.6 6.1 while.60
  331.8 5.2 while.61
  345.3 2.7 select_n.240
  350.4 2.6 broadcast.481
  353.1 2.7 broadcast.481.clone
  355.7 12.2 %while.60 = (s32[]{:T(128)}, f32[1,16,64,1152]{3,2,1,0:T(8,128)}, f32[1,16,64,1152]{3,2,1,0:T(8,128)}, f32[1,16,64]{2,1,0:T(8,128)S(1)}, f32[1,16,64]{2,1,0:T(8,...) while((s32[]{:T(128)}, f32[1,16,64,1152]{3,2,1,0:T(8,128)}, ...), condition=%wide.region_9.10_spmd, body=%wide.region_4.9_spmd.sunk | while | flops 187207856 | bytes 5385245 | solution.py:148
  368.0 10.4 while.61
  386.7 2.7 select_n.240
  391.8 2.6 broadcast.481
  394.4 2.7 broadcast.481.clone
  397.1 12.2 %while.60 = (s32[]{:T(128)}, f32[1,16,64,1152]{3,2,1,0:T(8,128)}, f32[1,16,64,1152]{3,2,1,0:T(8,128)}, f32[1,16,64]{2,1,0:T(8,128)S(1)}, f32[1,16,64]{2,1,0:T(8,...) while((s32[]{:T(128)}, f32[1,16,64,1152]{3,2,1,0:T(8,128)}, ...), condition=%wide.region_9.10_spmd, body=%wide.region_4.9_spmd.sunk | while | flops 187207856 | bytes 5385245 | solution.py:148
  409.3 10.4 while.61
  423.5 3.5 copy.25
  427.0 4.6 reshape_reshape.3
  431.7 6.4 copy.26
  438.2 632.5 %reduce-scatter.5.cloned.1.call-done = f32[128,28,64]{2,0,1:T(8,128)} async-done(((f32[256,28,64]{2,0,1:T(8,128)}), f32[128,28,64]{2,0,1:T(8,128)}) %reduce-scatter.5.cloned.1.call-update) | async-done | bytes 917520 | tf_op jit(solution)/shard_map/reduce_scatter | solution.py:26
  1070.8 32.7 %reduce-scatter.7.cloned.1.call-done = f32[32,28,64]{2,0,1:T(8,128)} async-done(((f32[128,28,64]{2,0,1:T(8,128)}), f32[32,28,64]{2,0,1:T(8,128)}) %reduce-scatter.7.cloned.1.call-update) | async-done | bytes 229392 | tf_op jit(solution)/shard_map/reduce_scatter | solution.py:26
  1106.5 74.0 %all-reduce.4.cloned.1.call-done = f32[32,28,64]{2,0,1:T(8,128)} async-done(((f32[32,28,64]{2,0,1:T(8,128)}), f32[32,28,64]{2,0,1:T(8,128)}) %all-reduce.4.cloned.1.call-update) | async-done | bytes 229392
  1181.4 17.5 %all-reduce.1 = f32[4,28,64]{2,0,1:T(4,128)S(1)} all-reduce(f32[4,28,64]{2,0,1:T(4,128)S(1)} %constant_dynamic-slice_fusion.3), channel_id=5, replica_groups=mesh['seq_0'=4,'seq_1'=8,'seq_2'=2,'grp'=4] {'grp'}, use_global_device_ids=true, to_apply=%region_20.22.clone | all-reduce | flops 7168 | bytes 57344
  (477 shorter events, 208.2 us)
Async XLA Ops:
  7.2 147.9 %copy-start = (bf16[1,128,7168]{2,1,0:T(8,128)(2,1)S(1)}, bf16[1,128,7168]{2,1,0:T(8,128)(2,1)}, u32[]{:S(2)}) copy-start(bf16[1,128,7168]{2,1,0:T(8,128)(2,1)} %param.16) | copy-start | bytes 5505028
  7.2 123.2 %collective-permute-start = (bf16[128,576]{0,1:T(8,128)(2,1)}, bf16[128,576]{0,1:T(8,128)(2,1)S(1)}, u32[]{:S(2)}, u32[]{:S(2)}) collective-permute-start(bf16[128,576]{0,1:T(8,128)(2,1)} %bitcast.275), channel_id=1, source_target_pairs={{0,32},{4,36},{8,40},{12,44},{16,48},{20,52},{24,56},{28,60},{32,6... | collective-permute-start | bytes 442376 | tf_op jit(solution)/shard_map/ppermute | solution.py:18
  16.4 116.6 %collective-permute-start.1 = (bf16[128,576]{0,1:T(8,128)(2,1)}, bf16[128,576]{0,1:T(8,128)(2,1)S(1)}, u32[]{:S(2)}, u32[]{:S(2)}) collective-permute-start(bf16[128,576]{0,1:T(8,128)(2,1)} %bitcast.276), channel_id=1, source_target_pairs={{0,28},{4,32},{8,36},{12,40},{16,44},{20,48},{24,52},{28,56},{32,6... | collective-permute-start | bytes 442376 | tf_op jit(solution)/shard_map/ppermute | solution.py:18
  19.4 116.2 %collective-permute-start.2 = (bf16[128,576]{0,1:T(8,128)(2,1)}, bf16[128,576]{0,1:T(8,128)(2,1)S(1)}, u32[]{:S(2)}, u32[]{:S(2)}) collective-permute-start(bf16[128,576]{0,1:T(8,128)(2,1)} %bitcast.277), channel_id=1, source_target_pairs={{0,24},{4,28},{8,32},{12,36},{16,40},{20,44},{24,48},{28,52},{32,5... | collective-permute-start | bytes 442376 | tf_op jit(solution)/shard_map/ppermute | solution.py:18
  22.4 116.0 %collective-permute-start.3 = (bf16[128,576]{0,1:T(8,128)(2,1)}, bf16[128,576]{0,1:T(8,128)(2,1)S(1)}, u32[]{:S(2)}, u32[]{:S(2)}) collective-permute-start(bf16[128,576]{0,1:T(8,128)(2,1)} %bitcast.278), channel_id=1, source_target_pairs={{0,20},{4,24},{8,28},{12,32},{16,36},{20,40},{24,44},{28,48},{32,5... | collective-permute-start | bytes 442376 | tf_op jit(solution)/shard_map/ppermute | solution.py:18
  29.6 22.9 %collective-permute-start.8 = (bf16[128,128]{1,0:T(8,128)(2,1)}, bf16[128,128]{1,0:T(8,128)(2,1)}, u32[]{:S(2)}, u32[]{:S(2)}) collective-permute-start(bf16[128,128]{1,0:T(8,128)(2,1)} %bitcast.285), channel_id=1, source_target_pairs={{0,32},{4,36},{8,40},{12,44},{16,48},{20,52},{24,56},{28,60},{32,6... | collective-permute-start | bytes 98312 | tf_op jit(solution)/shard_map/ppermute | solution.py:18
  34.6 16.2 %copy-start.4 = (s32[1,16]{1,0:T(1,128)S(1)}, s32[1,16]{1,0:T(1,128)}, u32[]{:S(2)}) copy-start(s32[1,16]{1,0:T(1,128)} %param.15) | copy-start | bytes 196
  34.6 18.0 %copy-start.3 = (bf16[1,128,128]{2,1,0:T(8,128)(2,1)S(1)}, bf16[1,128,128]{2,1,0:T(8,128)(2,1)}, u32[]{:S(2)}) copy-start(bf16[1,128,128]{2,1,0:T(8,128)(2,1)} %param.21) | copy-start | bytes 98308
  39.0 89.4 %copy-start.2 = (bf16[1,128,576]{1,2,0:T(8,128)(2,1)S(1)}, bf16[1,128,576]{1,2,0:T(8,128)(2,1)}, u32[]{:S(2)}) copy-start(bf16[1,128,576]{1,2,0:T(8,128)(2,1)} %param.19) | copy-start | bytes 442372
  39.0 109.8 %all-to-all-start = ((bf16[256,2,896]{2,1,0:T(2,128)(2,1)}), bf16[256,2,896]{2,1,0:T(2,128)(2,1)S(1)}, u32[]{:S(2)}, u32[]{:S(2)}) async-start(bf16[256,2,896]{2,1,0:T(2,128)(2,1)} %reshape.591), calls=%async_computation | async-start | bytes 1835008 | tf_op jit(solution)/shard_map/all_to_all | solution.py:204
  50.7 1020.0 %reduce-scatter.5.cloned.1.call-start = ((), (), s32[]{:S(2)}) async-start(), calls=%async_computation.3 | async-start | bytes 5505024 | tf_op jit(solution)/shard_map/reduce_scatter | solution.py:26
  52.5 24.8 %collective-permute-start.9 = (bf16[128,128]{1,0:T(8,128)(2,1)S(1)}, bf16[128,128]{1,0:T(8,128)(2,1)S(1)}, u32[]{:S(2)}, u32[]{:S(2)}) collective-permute-start(bf16[128,128]{1,0:T(8,128)(2,1)S(1)} %bitcast.286), channel_id=1, source_target_pairs={{0,28},{4,32},{8,36},{12,40},{16,44},{20,48},{24,52},{28,56},{32,6... | collective-permute-start | bytes 98312 | tf_op jit(solution)/shard_map/ppermute | solution.py:18
  77.3 9.7 collective-permute-start.10
  87.0 9.1 collective-permute-start.11
  96.1 8.8 collective-permute-start.12
  104.9 8.2 collective-permute-start.13
  113.2 7.9 collective-permute-start.14
  121.1 7.3 collective-permute-start.15
  128.4 12.9 %collective-permute-start.4 = (bf16[128,576]{0,1:T(8,128)(2,1)S(1)}, bf16[128,576]{0,1:T(8,128)(2,1)S(1)}, u32[]{:S(2)}, u32[]{:S(2)}) collective-permute-start(bf16[128,576]{0,1:T(8,128)(2,1)S(1)} %bitcast.279), channel_id=1, source_target_pairs={{0,16},{4,20},{8,24},{12,28},{16,32},{20,36},{24,40},{28,44},{32,4... | collective-permute-start | bytes 442376 | tf_op jit(solution)/shard_map/ppermute | solution.py:18
  130.4 17.8 %copy-start.1 = (bf16[1280,128]{1,0:T(8,128)(2,1)}, bf16[1280,128]{1,0:T(8,128)(2,1)S(1)}, u32[]{:S(2)}) copy-start(bf16[1280,128]{1,0:T(8,128)(2,1)S(1)} %constant_dynamic-update-slice_fusion.10) | copy-start | bytes 983044
  130.4 12.1 %collective-permute-start.5 = (bf16[128,576]{0,1:T(8,128)(2,1)S(1)}, bf16[128,576]{0,1:T(8,128)(2,1)S(1)}, u32[]{:S(2)}, u32[]{:S(2)}) collective-permute-start(bf16[128,576]{0,1:T(8,128)(2,1)S(1)} %bitcast.280), channel_id=1, source_target_pairs={{0,12},{4,16},{8,20},{12,24},{16,28},{20,32},{24,36},{28,40},{32,4... | collective-permute-start | bytes 442376 | tf_op jit(solution)/shard_map/ppermute | solution.py:18
  133.0 12.8 %collective-permute-start.6 = (bf16[128,576]{0,1:T(8,128)(2,1)S(1)}, bf16[128,576]{0,1:T(8,128)(2,1)S(1)}, u32[]{:S(2)}, u32[]{:S(2)}) collective-permute-start(bf16[128,576]{0,1:T(8,128)(2,1)S(1)} %bitcast.281), channel_id=1, source_target_pairs={{0,8},{4,12},{8,16},{12,20},{16,24},{20,28},{24,32},{28,36},{32,40... | collective-permute-start | bytes 442376 | tf_op jit(solution)/shard_map/ppermute | solution.py:18
  135.7 11.2 collective-permute-start.7
  438.1 665.4 %copy-start.6 = (u32[256]{0:T(256)S(1)}, u32[256]{0:T(256)}, u32[]{:S(2)}) copy-start(u32[256]{0:T(256)} %constant.381) | copy-start | bytes 3076
  438.1 666.0 %copy-start.5 = (u32[256]{0:T(256)S(1)}, u32[256]{0:T(256)}, u32[]{:S(2)}) copy-start(u32[256]{0:T(256)} %constant.385) | copy-start | bytes 3076
  438.1 665.3 %reduce-scatter.7.cloned.1.call-start = ((), (), s32[]{:S(2)}) async-start(), calls=%async_computation.4 | async-start | bytes 2293760 | tf_op jit(solution)/shard_map/reduce_scatter | solution.py:26
  1070.7 109.7 %all-reduce.4.cloned.1.call-start = ((), (), s32[]{:S(2)}) async-start(), calls=%async_computation.5 | async-start | bytes 917504
Sparse Core Ops, SparseCore 0:
  438.2 632.4 reduce-scatter.4
  1073.2 30.1 reduce-scatter.6
  1105.8 74.6 all-reduce.3
